TPU v7x, 128 devices: a whole 4x4x4 slice. The times are simulated.
128 devices in a mesh: grp: 8 (over x, core), dev: 16 (over y, z).
Axes of the slice: x: 4, y: 4, z: 4, core: 2. Of those that a mesh axis runs over, the one named last changes fastest.
Arguments:
- parent_state: float32 [24, 512, 2048], P(None, 'grp', 'dev'), may hold values from -6 to 6
- nest_state: float32 [16, 24, 384, 384], P('grp', None, 'dev'), may hold values from -6 to 6
- nest_anchor: int32 [16, 2], replicated, may hold values from 0 to 1920, as said below
- diffusion: float32 [2, 24], replicated, may hold values from 0.02 to 0.05
- courant: float32 [2, 24], replicated, may hold values from 0.05 to 0.15
Outputs:
- parent_out: float32 [24, 512, 2048], P(None, 'grp', 'dev')
- nest_out: float32 [16, 24, 384, 384], P('grp', None, 'dev')
Inputs may be any that keep to these rules, and one draw needn't show every extreme that they name: `nest_anchor`: the parent grid is cut into 2 x 16 / 2 disjoint bands of 256 x 256 cells; each nest lies in a band of its own, its 128 x 128 covered cells inside that band.
All inputs are finite; a program needn't handle non-finite values.
Results may differ from a plain program's by a relative error of at most 0.0003.
Values sent between devices are 32-bit elements; how exact they have to be, the bound alone decides.
A program may use at most 320 MiB of HBM per device.

v0:
```python
import jax
import jax.numpy as jnp
from jax import lax
from jax.sharding import PartitionSpec as P


def padded_2(shard, sides, width):
    for axis, dim in sides:
        size, length = (lax.axis_size(axis), shard.shape[dim])
        up = [(i, (i + 1) % size) for i in range(size - 1)]
        down = [(j, i) for i, j in up]
        last = lax.slice_in_dim(shard, length - width, length, axis=dim)
        initial = lax.slice_in_dim(shard, 0, width, axis=dim)
        before = lax.ppermute(last, axis, up)
        after = lax.ppermute(initial, axis, down)
        shard = jnp.concatenate([before, shard, after], axis=dim)
    return shard


def stencil(padded, diff_x, diff_y, adv_x, adv_y):
    centre = padded[..., 1:-1, 1:-1]
    eastern = padded[..., 1:-1, 2:]
    western = padded[..., 1:-1, :-2]
    northern = padded[..., 2:, 1:-1]
    southern = padded[..., :-2, 1:-1]
    return (
        centre
        + diff_x * (eastern - 2.0 * centre + western)
        + diff_y * (northern - 2.0 * centre + southern)
        - adv_x * (centre - western)
        - adv_y * (centre - southern)
    )


def impose(extended, row_index, south_fine, north_fine, total_rows):
    below = (row_index < 0)[None, None, :, None]
    above = (row_index >= total_rows)[None, None, :, None]
    extended = jnp.where(below, south_fine[:, :, None, :], extended)
    return jnp.where(above, north_fine[:, :, None, :], extended)


def substep_once(
    extended, row_index, west_full, east_full, south_fine, north_fine, total_rows, coefficients
):
    row_count = extended.shape[2]
    first_row = row_index[0] + 3
    west_col = lax.dynamic_slice_in_dim(west_full, first_row, row_count, 2)
    east_col = lax.dynamic_slice_in_dim(east_full, first_row, row_count, 2)
    padded = jnp.concatenate([west_col[..., None], extended, east_col[..., None]], axis=3)
    advanced = stencil(padded, coefficients[0], coefficients[1], coefficients[2], coefficients[3])
    inner_rows = row_index[1:-1]
    return (impose(advanced, inner_rows, south_fine, north_fine, total_rows), inner_rows)


def shards(parent_state, nest_state, nest_anchor, diffusion, courant):
    channels, tile_rows, tile_cols = parent_state.shape
    local_nests = nest_state.shape[0]
    nest_rows_dev = nest_state.shape[2]
    fine_cols = nest_state.shape[3]
    dev_count = lax.axis_size("dev")
    grp_index = lax.axis_index("grp")
    dev_index = lax.axis_index("dev")
    total_rows = nest_rows_dev * dev_count
    foot_rows = total_rows // 3
    foot_cols = fine_cols // 3
    nest_count = nest_anchor.shape[0]
    diff_x = diffusion[0][:, None, None]
    diff_y = diffusion[1][:, None, None]
    adv_x = courant[0][:, None, None]
    adv_y = courant[1][:, None, None]
    nest_coefficients = (3.0 * diff_x, 3.0 * diff_y, adv_x, adv_y)
    row_base = grp_index * tile_rows
    col_base = dev_index * tile_cols
    highest = lax.Precision.HIGHEST
    row_anchor = nest_anchor[:, 0:1]
    col_anchor = nest_anchor[:, 1:2]
    along_rows = jnp.arange(foot_rows, dtype=jnp.int32)[None, :]
    along_cols = jnp.arange(foot_cols, dtype=jnp.int32)[None, :]
    rows_here = row_base + jnp.arange(tile_rows, dtype=jnp.int32)
    cols_here = col_base + jnp.arange(tile_cols, dtype=jnp.int32)
    side_cols = jnp.concatenate([col_anchor - 1, col_anchor + foot_cols], axis=0)
    column_pick = (side_cols == cols_here[None, :]).astype(jnp.float32)
    column_values = jnp.einsum("cyx,mx->cym", parent_state, column_pick, precision=highest)
    row_span = ((row_anchor + along_rows)[:, :, None] == rows_here[None, None, :]).astype(
        jnp.float32
    )
    west_part = jnp.einsum(
        "nky,cyn->cnk", row_span, column_values[:, :, :nest_count], precision=highest
    )
    east_part = jnp.einsum(
        "nky,cyn->cnk", row_span, column_values[:, :, nest_count:], precision=highest
    )
    side_rows = jnp.concatenate([row_anchor - 1, row_anchor + foot_rows], axis=0)
    row_pick = (side_rows == rows_here[None, :]).astype(jnp.float32)
    row_values = jnp.einsum("my,cyx->cmx", row_pick, parent_state, precision=highest)
    col_span = ((col_anchor + along_cols)[:, :, None] == cols_here[None, None, :]).astype(
        jnp.float32
    )
    south_part = jnp.einsum("nkx,cnx->cnk", col_span, row_values[:, :nest_count], precision=highest)
    north_part = jnp.einsum("nkx,cnx->cnk", col_span, row_values[:, nest_count:], precision=highest)
    contrib = jnp.concatenate([west_part, east_part, south_part, north_part], axis=2)
    cycle_every = lax.psum(contrib, ("grp", "dev"))
    cycle_local = lax.dynamic_slice_in_dim(cycle_every, grp_index * local_nests, local_nests, 1)
    cycle_local = jnp.swapaxes(cycle_local, 0, 1)
    west_fine = jnp.repeat(cycle_local[:, :, :foot_rows], 3, axis=2)
    east_fine = jnp.repeat(cycle_local[:, :, foot_rows : 2 * foot_rows], 3, axis=2)
    west_full = jnp.pad(west_fine, ((0, 0), (0, 0), (3, 3)), mode="edge")
    east_full = jnp.pad(east_fine, ((0, 0), (0, 0), (3, 3)), mode="edge")
    south_fine = jnp.repeat(cycle_local[:, :, 2 * foot_rows : 2 * foot_rows + foot_cols], 3, axis=2)
    north_fine = jnp.repeat(cycle_local[:, :, 2 * foot_rows + foot_cols :], 3, axis=2)
    parent_pad = padded_2(parent_state, (("grp", 1), ("dev", 2)), 1)
    advanced = stencil(parent_pad, diff_x, diff_y, adv_x, adv_y)
    current = nest_state
    for substep in range(3):
        extended = padded_2(current, (("dev", 2),), 1)
        row_index = dev_index * nest_rows_dev - 1 + jnp.arange(nest_rows_dev + 2, dtype=jnp.int32)
        extended = impose(extended, row_index, south_fine, north_fine, total_rows)
        current = substep_once(
            extended,
            row_index,
            west_full,
            east_full,
            south_fine,
            north_fine,
            total_rows,
            nest_coefficients,
        )[0]
    coarse_rows = nest_rows_dev // 3
    averages = current.reshape(local_nests, channels, coarse_rows, 3, foot_cols, 3).mean(
        axis=(3, 5)
    )
    per_group = local_nests * dev_count
    zero_start = jnp.zeros((), jnp.int32)
    canvas = jnp.pad(advanced, ((0, 0), (coarse_rows, coarse_rows), (foot_cols, foot_cols)))
    pieces = lax.all_gather(averages, ("grp", "dev"), axis=0, tiled=True)
    item_count = pieces.shape[0]

    def put_one(item, canvas_inner):
        group_index = item // per_group
        member = item // local_nests % dev_count
        nest_index = group_index * local_nests + item % local_nests
        anchor = lax.dynamic_slice(nest_anchor, (nest_index, zero_start), (1, 2))
        top_at = jnp.clip(
            anchor[0, 0] + member * coarse_rows - row_base + coarse_rows, 0, tile_rows + coarse_rows
        )
        left_at = jnp.clip(anchor[0, 1] - col_base + foot_cols, 0, tile_cols + foot_cols)
        piece = lax.dynamic_index_in_dim(pieces, item, 0, keepdims=False)
        return lax.dynamic_update_slice(canvas_inner, piece, (zero_start, top_at, left_at))

    filled = lax.fori_loop(0, item_count, put_one, canvas)
    parent_out = filled[:, coarse_rows : coarse_rows + tile_rows, foot_cols : foot_cols + tile_cols]
    return (parent_out, current)


def solution(mesh):
    placed = (P(None, "grp", "dev"), P("grp", None, "dev", None), P(), P(), P())
    return jax.shard_map(
        shards,
        mesh=mesh,
        in_specs=placed,
        out_specs=(P(None, "grp", "dev"), P("grp", None, "dev", None)),
        check_vma=False,
    )
```

profile of v0, /device:TPU:95, one launch (start us, length us, event | category | flops | bytes accessed | tf_op | source)
XLA Modules:
  0.0 2034.9 jit_solution(8243158186074569799)
XLA Ops:
  22.1 138.1 %all-reduce.3.cloned.1.call-done = f32[24,16,512]{2,0,1:T(8,128)} async-done(((f32[24,16,512]{2,0,1:T(8,128)}), f32[24,16,512]{2,0,1:T(8,128)}) %all-reduce.3.cloned.1.call-update) | async-done | bytes 786448 | tf_op jit(solution)/shard_map/psum | solution.py:102
  188.6 8.9 copy.162
  197.5 10.2 reduce_sum.9
  238.1 72.8 %all-gather.2.cloned.1.call-done = f32[256,24,8,128]{3,2,1,0:T(8,128)} async-done(((f32[2,24,8,128]{3,2,1,0:T(8,128)}), f32[256,24,8,128]{3,2,1,0:T(8,128)}) %all-gather.2.cloned.1.call-update) | async-done | bytes 25165840 | tf_op jit(solution)/shard_map/all_gather | solution.py:135
  310.9 1715.1 %while.16 = (s32[]{:T(128)}, f32[24,80,384]{2,1,0:T(8,128)}, f32[256,24,8,128]{3,2,1,0:T(8,128)}, s32[16,2]{0,1:T(2,128)S(1)}, s32[]{:T(128)}, /*index=5*/s32[]{...) while((s32[]{:T(128)}, f32[24,80,384]{2,1,0:T(8,128)}, ...), condition=%wide.region_3.4_spmd, body=%wide.region_2.3_spmd.sunk | while | flops 46 | bytes 393896 | solution.py:150
  505.9 8.7 dynamic_update_slice.12
  541.0 8.7 dynamic_update_slice.12
  576.1 8.7 dynamic_update_slice.12
  611.2 8.7 dynamic_update_slice.12
  628.8 8.7 dynamic_update_slice.12
  646.3 8.7 dynamic_update_slice.12
  663.9 8.7 dynamic_update_slice.12
  681.4 8.7 dynamic_update_slice.12
  699.0 8.7 dynamic_update_slice.12
  716.6 8.7 dynamic_update_slice.12
  984.8 8.7 dynamic_update_slice.12
  1020.0 8.7 dynamic_update_slice.12
  1037.5 8.7 dynamic_update_slice.12
  1055.1 8.7 dynamic_update_slice.12
  1072.6 8.7 dynamic_update_slice.12
  1090.2 8.7 dynamic_update_slice.12
  1107.7 8.7 dynamic_update_slice.12
  1125.3 8.7 dynamic_update_slice.12
  1142.8 8.7 dynamic_update_slice.12
  (1112 shorter events, 1293.3 us)
Async XLA Ops:
  7.2 4.3 copy-start
  7.2 153.0 %all-reduce.3.cloned.1.call-start = ((), (), s32[]{:S(2)}) async-start(), calls=%async_computation | async-start | bytes 1572864 | tf_op jit(solution)/shard_map/psum | solution.py:102
  11.9 3.1 copy-start.4
  14.9 7.1 copy-start.7
  14.9 7.2 copy-start.6
  14.9 295.9 %all-gather.2.cloned.1.call-start = ((), (), s32[]{:S(2)}) async-start(), calls=%async_computation.1 | async-start | bytes 25362432 | tf_op jit(solution)/shard_map/all_gather | solution.py:135
  15.3 1.2 copy-start.3
  16.5 147.4 %collective-permute-start.4 = (f32[2,24,1,384]{3,1,2,0:T(8,128)S(1)}, f32[2,24,1,384]{3,1,2,0:T(8,128)S(1)}, u32[]{:S(2)}, u32[]{:S(2)}) collective-permute-start(f32[2,24,1,384]{3,1,2,0:T(8,128)S(1)} %get-tuple-element.229), channel_id=1, source_target_pairs={{0,1},{1,2},{2,3},{3,4},{4,5},{5,6},{6,7},{7,8},{8,9},{9,10},{10,1... | collective-permute-start | bytes 221192 | tf_op jit(solution)/shard_map/ppermute | solution.py:14
  19.8 144.1 %collective-permute-start.5 = (f32[2,24,1,384]{3,1,2,0:T(8,128)S(1)}, f32[2,24,1,384]{3,1,2,0:T(8,128)S(1)}, u32[]{:S(2)}, u32[]{:S(2)}) collective-permute-start(f32[2,24,1,384]{3,1,2,0:T(8,128)S(1)} %get-tuple-element.230), channel_id=1, source_target_pairs={{1,0},{2,1},{3,2},{4,3},{5,4},{6,5},{7,6},{8,7},{9,8},{10,9},{11,1... | collective-permute-start | bytes 221192 | tf_op jit(solution)/shard_map/ppermute | solution.py:15
  163.9 12.5 copy-start.1
  168.2 5.8 collective-permute-start.6
  171.0 5.1 collective-permute-start.7
  178.6 5.6 collective-permute-start.8
  180.5 5.9 copy-start.2
  180.6 5.5 collective-permute-start.9
  210.0 6.6 collective-permute-start
  211.3 6.1 collective-permute-start.1
  220.5 10.5 collective-permute-start.2
  224.2 6.4 collective-permute-start.3
  236.5 74.3 %copy-start.5 = (s32[16,2]{0,1:T(2,128)S(1)}, s32[16,2]{0,1:T(2,128)}, u32[]{:S(2)}) copy-start(s32[16,2]{0,1:T(2,128)} %param.9) | copy-start | bytes 388
Sparse Core Ops, SparseCore 0:
  15.0 145.1 all-reduce.2
  210.1 100.7 all-gather.1
where the time goes:
time: 2070 us; the launch traced here: 2030 us
  local copies, waits for them, and re-layouts  1410 us (68%)
  loops' own time  332 us (16%)
  waiting for transfers between devices  221 us (11%)
  starting transfers between devices  28.4 us (1%)
  other arithmetic  24.7 us (1%)
    dynamic_update_slice x256, local copies, waits for them, and re-layouts, put_one(): lax.dynamic_update_slice(canvas_inner, piece, (zero_start, top_at, left_at))  985 us
    another operation x1, loops' own time, shards(): filled = lax.fori_loop(0, item_count, put_one, canvas)  332 us
    squeeze x256, local copies, waits for them, and re-layouts, put_one(): piece = lax.dynamic_index_in_dim(pieces, item, 0, keepdims=False)  232 us
    slice x256, local copies, waits for them, and re-layouts, put_one(): anchor[0, 1] - col_base + foot_cols  148 us
    psum x1, waiting for transfers between devices, shards(): cycle_every = lax.psum(contrib, ('grp', 'dev'))  138 us
    all_gather x1, waiting for transfers between devices, shards(): pieces = lax.all_gather(averages, ('grp', 'dev'), axis=0, tiled=True)  72.8 us
  transfers between devices with their start and end apart: 12, of which 7 were waited for; matrix products, arithmetic and copies ran while one was open for 1% of the time, Pallas kernels for 0%

commit v1 on v0

--- a/solution.py
+++ b/solution.py
@@ -99,7 +99,7 @@
     south_part = jnp.einsum("nkx,cnx->cnk", col_span, row_values[:, :nest_count], precision=highest)
     north_part = jnp.einsum("nkx,cnx->cnk", col_span, row_values[:, nest_count:], precision=highest)
     contrib = jnp.concatenate([west_part, east_part, south_part, north_part], axis=2)
-    cycle_every = lax.psum(contrib, ("grp", "dev"))
+    cycle_every = jnp.sum(lax.all_gather(contrib, ("grp", "dev")), axis=0)
     cycle_local = lax.dynamic_slice_in_dim(cycle_every, grp_index * local_nests, local_nests, 1)
     cycle_local = jnp.swapaxes(cycle_local, 0, 1)
     west_fine = jnp.repeat(cycle_local[:, :, :foot_rows], 3, axis=2)

time: 2070 us -> 2170 us (1.048)
  waiting for transfers between devices: 221 us -> 296 us
  other arithmetic: 24.7 us -> 55.6 us
    all_gather x0 -> x1, waiting for transfers between devices: none -> 216 us  [shards(): cycle_every = jnp.sum(lax.all_gather(contrib, ('grp', 'dev')), axis=0)]
    psum x1 -> x0, waiting for transfers between devices: 138 us -> none  [shards(): cycle_every = lax.psum(contrib, ('grp', 'dev'))]
    reduce_sum x0 -> x1, other arithmetic: none -> 30.6 us  [shards(): cycle_every = jnp.sum(lax.all_gather(contrib, ('grp', 'dev')), axis=0)]
  transfers between devices with their start and end apart: 12 -> 12, of which waited for: 7 -> 7; matrix products, arithmetic and copies ran while one was open for 1% -> 2% of each run, Pallas kernels for 0% -> 0%
where the time goes in v1:
time: 2170 us; the launch traced here: 2130 us
  local copies, waits for them, and re-layouts  1400 us (65%)
  loops' own time  334 us (15%)
  waiting for transfers between devices  296 us (14%)
  other arithmetic  55.6 us (3%)
  starting transfers between devices  28.2 us (1%)
    dynamic_update_slice x256, local copies, waits for them, and re-layouts, put_one(): lax.dynamic_update_slice(canvas_inner, piece, (zero_start, top_at, left_at))  985 us
    another operation x1, loops' own time, shards(): filled = lax.fori_loop(0, item_count, put_one, canvas)  334 us
    squeeze x256, local copies, waits for them, and re-layouts, put_one(): piece = lax.dynamic_index_in_dim(pieces, item, 0, keepdims=False)  232 us
    all_gather x1, waiting for transfers between devices, shards(): cycle_every = jnp.sum(lax.all_gather(contrib, ('grp', 'dev')), axis=0)  216 us
    slice x256, local copies, waits for them, and re-layouts, put_one(): anchor[0, 1] - col_base + foot_cols  138 us
    all_gather x1, waiting for transfers between devices, shards(): pieces = lax.all_gather(averages, ('grp', 'dev'), axis=0, tiled=True)  71 us
  transfers between devices with their start and end apart: 12, of which 7 were waited for; matrix products, arithmetic and copies ran while one was open for 2% of the time, Pallas kernels for 0%

profile of v1, /device:TPU:95, one launch (start us, length us, event | category | flops | bytes accessed | tf_op | source)
XLA Modules:
  0.0 2134.6 jit_solution(7152141047967232105)
XLA Ops:
  22.0 216.2 %all-gather.6.cloned.1.call-done = f32[3072,16,512]{2,0,1:T(8,128)} async-done(((f32[24,16,512]{2,0,1:T(8,128)}), f32[3072,16,512]{2,0,1:T(8,128)}) %all-gather.6.cloned.1.call-update) | async-done | bytes 100663312 | tf_op jit(solution)/shard_map/all_gather | solution.py:102
  238.2 30.6 %reduce_sum.18 = f32[24,16,512]{2,0,1:T(8,128)S(1)} reduce(f32[128,24,16,512]{3,1,0,2:T(8,128)} %bitcast.23, f32[]{:T(128)} %constant.219.clone.1), dimensions={0}, to_apply=%region_0.0 | reduce | flops 24969216 | bytes 101449728 | tf_op jit(solution)/shard_map/reduce_sum | solution.py:102
  296.8 8.9 copy.158
  305.7 10.2 reduce_sum.19
  347.9 71.0 %all-gather.4.cloned.1.call-done = f32[256,24,8,128]{3,2,1,0:T(8,128)} async-done(((f32[2,24,8,128]{3,2,1,0:T(8,128)}), f32[256,24,8,128]{3,2,1,0:T(8,128)}) %all-gather.4.cloned.1.call-update) | async-done | bytes 25165840 | tf_op jit(solution)/shard_map/all_gather | solution.py:135
  418.9 1706.7 %while.16 = (s32[]{:T(128)}, f32[24,80,384]{2,1,0:T(8,128)}, f32[256,24,8,128]{3,2,1,0:T(8,128)}, s32[16,2]{0,1:T(2,128)S(1)}, s32[]{:T(128)}, /*index=5*/s32[]{...) while((s32[]{:T(128)}, f32[24,80,384]{2,1,0:T(8,128)}, ...), condition=%wide.region_3.4_spmd, body=%wide.region_2.3_spmd.sunk | while | flops 46 | bytes 393888 | solution.py:150
  612.8 8.7 dynamic_update_slice.12
  630.3 8.7 dynamic_update_slice.12
  665.3 8.7 dynamic_update_slice.12
  682.8 8.7 dynamic_update_slice.12
  717.8 8.7 dynamic_update_slice.12
  735.3 8.7 dynamic_update_slice.12
  770.3 8.7 dynamic_update_slice.12
  787.7 8.7 dynamic_update_slice.12
  805.2 8.7 dynamic_update_slice.12
  822.7 8.7 dynamic_update_slice.12
  1089.7 8.7 dynamic_update_slice.12
  1124.7 8.7 dynamic_update_slice.12
  1142.1 8.7 dynamic_update_slice.12
  1177.1 8.7 dynamic_update_slice.12
  1194.6 8.7 dynamic_update_slice.12
  1212.1 8.7 dynamic_update_slice.12
  1229.6 8.7 dynamic_update_slice.12
  1247.1 8.7 dynamic_update_slice.12
  (1113 shorter events, 1292.8 us)
Async XLA Ops:
  7.2 4.3 copy-start
  7.2 231.0 %all-gather.6.cloned.1.call-start = ((), (), s32[]{:S(2)}) async-start(), calls=%async_computation.1 | async-start | bytes 101449728 | tf_op jit(solution)/shard_map/all_gather | solution.py:102
  11.9 3.1 copy-start.4
  14.9 7.1 copy-start.7
  14.9 7.1 copy-start.6
  14.9 404.0 %all-gather.4.cloned.1.call-start = ((), (), s32[]{:S(2)}) async-start(), calls=%async_computation | async-start | bytes 25362432 | tf_op jit(solution)/shard_map/all_gather | solution.py:135
  15.3 1.2 copy-start.3
  16.5 255.2 %collective-permute-start.4 = (f32[2,24,1,384]{3,1,2,0:T(8,128)S(1)}, f32[2,24,1,384]{3,1,2,0:T(8,128)S(1)}, u32[]{:S(2)}, u32[]{:S(2)}) collective-permute-start(f32[2,24,1,384]{3,1,2,0:T(8,128)S(1)} %get-tuple-element.229), channel_id=1, source_target_pairs={{0,1},{1,2},{2,3},{3,4},{4,5},{5,6},{6,7},{7,8},{8,9},{9,10},{10,1... | collective-permute-start | bytes 221192 | tf_op jit(solution)/shard_map/ppermute | solution.py:14
  19.8 252.0 %collective-permute-start.5 = (f32[2,24,1,384]{3,1,2,0:T(8,128)S(1)}, f32[2,24,1,384]{3,1,2,0:T(8,128)S(1)}, u32[]{:S(2)}, u32[]{:S(2)}) collective-permute-start(f32[2,24,1,384]{3,1,2,0:T(8,128)S(1)} %get-tuple-element.230), channel_id=1, source_target_pairs={{1,0},{2,1},{3,2},{4,3},{5,4},{6,5},{7,6},{8,7},{9,8},{10,9},{11,1... | collective-permute-start | bytes 221192 | tf_op jit(solution)/shard_map/ppermute | solution.py:15
  271.7 12.8 copy-start.1
  276.0 5.5 collective-permute-start.6
  279.1 5.1 collective-permute-start.7
  286.8 5.6 collective-permute-start.8
  288.7 5.9 copy-start.2
  288.7 5.5 collective-permute-start.9
  318.1 6.4 collective-permute-start
  319.4 5.9 collective-permute-start.1
  328.4 7.1 collective-permute-start.2
  333.5 7.0 collective-permute-start.3
  346.4 72.5 %copy-start.5 = (s32[16,2]{0,1:T(2,128)S(1)}, s32[16,2]{0,1:T(2,128)}, u32[]{:S(2)}) copy-start(s32[16,2]{0,1:T(2,128)} %param.9) | copy-start | bytes 388
Sparse Core Ops, SparseCore 0:
  15.0 223.1 all-gather.5
  318.2 100.6 all-gather.3

commit v2 on v0

--- a/solution.py
+++ b/solution.py
@@ -132,7 +132,10 @@
     per_group = local_nests * dev_count
     zero_start = jnp.zeros((), jnp.int32)
     canvas = jnp.pad(advanced, ((0, 0), (coarse_rows, coarse_rows), (foot_cols, foot_cols)))
-    pieces = lax.all_gather(averages, ("grp", "dev"), axis=0, tiled=True)
+    pieces = jnp.concatenate(
+        lax.all_to_all(jnp.stack([averages] * lax.axis_size(("grp", "dev"))), ("grp", "dev"), 0, 0),
+        axis=0,
+    )
     item_count = pieces.shape[0]
 
     def put_one(item, canvas_inner):

time: 2070 us -> 2340 us (1.13)
  the two profiles are of different devices: /device:TPU:95 before, /device:TPU:127 now
where the time goes in v2:
time: 2340 us; the launch traced here: 2310 us
  local copies, waits for them, and re-layouts  1410 us (60%)
  waiting for transfers between devices  493 us (21%)
  loops' own time  310 us (13%)
  starting transfers between devices  44.7 us (2%)
  other arithmetic  24 us (1%)
    dynamic_update_slice x256, local copies, waits for them, and re-layouts, put_one(): lax.dynamic_update_slice(canvas_inner, piece, (zero_start, top_at, left_at))  987 us
    another operation x1, loops' own time, shards(): filled = lax.fori_loop(0, item_count, put_one, canvas)  310 us
    squeeze x256, local copies, waits for them, and re-layouts, put_one(): piece = lax.dynamic_index_in_dim(pieces, item, 0, keepdims=False)  232 us
    all_to_all x1, waiting for transfers between devices, shards(): lax.all_to_all(jnp.stack([averages] * lax.axis_size(('grp', 'dev'))), ('g...  209 us
    ppermute x5, waiting for transfers between devices, padded_2(): after = lax.ppermute(initial, axis, down)  146 us
    slice x256, local copies, waits for them, and re-layouts, put_one(): anchor[0, 1] - col_base + foot_cols  139 us
    psum x1, waiting for transfers between devices, shards(): cycle_every = lax.psum(contrib, ('grp', 'dev'))  138 us
  transfers between devices with their start and end apart: 12, of which 6 were waited for; matrix products, arithmetic and copies ran while one was open for 1% of the time, Pallas kernels for 0%

profile of v2, /device:TPU:127, one launch (start us, length us, event | category | flops | bytes accessed | tf_op | source)
XLA Modules:
  0.0 2305.8 jit_solution(6446013359117400977)
XLA Ops:
  22.0 137.7 %all-reduce.3.cloned.1.call-done = f32[24,16,512]{2,0,1:T(8,128)} async-done(((f32[24,16,512]{2,0,1:T(8,128)}), f32[24,16,512]{2,0,1:T(8,128)}) %all-reduce.3.cloned.1.call-update) | async-done | bytes 786448 | tf_op jit(solution)/shard_map/psum | solution.py:102
  186.7 8.8 copy.162
  195.4 10.2 reduce_sum.9
  207.2 11.5 stack.2
  218.7 20.1 all-to-all-start
  250.9 142.9 %collective-permute-done.2 = f32[24,66,1]{1,0,2:T(8,128)S(1)} collective-permute-done((f32[24,66,1]{1,0,2:T(8,128)S(1)}, f32[24,66,1]{1,0,2:T(8,128)S(1)}, u32[]{:S(2)}, u32[]{:S(2)}) %collective-permute-start.2) | collective-permute-done | bytes 6368 | tf_op jit(solution)/shard_map/ppermute | solution.py:15
  401.1 208.5 %all-to-all-done = f32[128,2,24,8,128]{4,3,2,1,0:T(8,128)} async-done(((f32[128,2,24,8,128]{4,3,2,1,0:T(8,128)}), f32[128,2,24,8,128]{4,3,2,1,0:T(8,128)}, u32[]{:S(2)}, u32[]{:S(2)}) %all-to-all-start) | async-done | bytes 25165856 | tf_op jit(solution)/shard_map/all_to_all | solution.py:136
  609.7 1687.2 %while.16 = (s32[]{:T(128)}, f32[24,80,384]{2,1,0:T(8,128)}, f32[256,24,8,128]{3,2,1,0:T(8,128)}, s32[16,2]{0,1:T(2,128)S(1)}, s32[]{:T(128)}, /*index=5*/s32[]{...) while((s32[]{:T(128)}, f32[24,80,384]{2,1,0:T(8,128)}, ...), condition=%wide.region_3.4_spmd, body=%wide.region_2.3_spmd.sunk | while | flops 46 | bytes 393888 | solution.py:153
  801.4 8.6 dynamic_update_slice.12
  818.7 8.6 dynamic_update_slice.12
  836.0 8.6 dynamic_update_slice.12
  853.3 8.6 dynamic_update_slice.12
  870.5 8.6 dynamic_update_slice.12
  887.8 8.6 dynamic_update_slice.12
  905.1 8.6 dynamic_update_slice.12
  939.7 8.6 dynamic_update_slice.12
  956.9 8.6 dynamic_update_slice.12
  974.2 8.6 dynamic_update_slice.12
  991.5 8.6 dynamic_update_slice.12
  1008.8 8.6 dynamic_update_slice.12
  1026.1 8.7 dynamic_update_slice.12
  1043.4 8.7 dynamic_update_slice.12
  1272.9 8.6 dynamic_update_slice.12
  1290.1 8.6 dynamic_update_slice.12
  (1112 shorter events, 1302.7 us)
Async XLA Ops:
  7.2 4.3 copy-start
  7.2 152.6 %all-reduce.3.cloned.1.call-start = ((), (), s32[]{:S(2)}) async-start(), calls=%async_computation.1 | async-start | bytes 1572864 | tf_op jit(solution)/shard_map/psum | solution.py:102
  11.9 3.0 copy-start.4
  14.9 7.0 copy-start.7
  14.9 7.1 copy-start.6
  15.3 1.2 copy-start.3
  16.5 147.0 %collective-permute-start.4 = (f32[2,24,1,384]{3,1,2,0:T(8,128)S(1)}, f32[2,24,1,384]{3,1,2,0:T(8,128)S(1)}, u32[]{:S(2)}, u32[]{:S(2)}) collective-permute-start(f32[2,24,1,384]{3,1,2,0:T(8,128)S(1)} %get-tuple-element.229), channel_id=1, source_target_pairs={{0,1},{1,2},{2,3},{3,4},{4,5},{5,6},{6,7},{7,8},{8,9},{9,10},{10,1... | collective-permute-start | bytes 221192 | tf_op jit(solution)/shard_map/ppermute | solution.py:14
  17.8 145.7 %collective-permute-start.5 = (f32[2,24,1,384]{3,1,2,0:T(8,128)S(1)}, f32[2,24,1,384]{3,1,2,0:T(8,128)S(1)}, u32[]{:S(2)}, u32[]{:S(2)}) collective-permute-start(f32[2,24,1,384]{3,1,2,0:T(8,128)S(1)} %get-tuple-element.230), channel_id=1, source_target_pairs={{1,0},{2,1},{3,2},{4,3},{5,4},{6,5},{7,6},{8,7},{9,8},{10,9},{11,1... | collective-permute-start | bytes 221192 | tf_op jit(solution)/shard_map/ppermute | solution.py:15
  163.5 11.3 copy-start.1
  167.7 5.3 collective-permute-start.6
  169.0 5.4 collective-permute-start.7
  177.0 6.0 collective-permute-start.8
  178.3 6.2 copy-start.2
  178.3 5.9 collective-permute-start.9
  218.7 391.0 %all-to-all-start = ((f32[128,2,24,8,128]{4,3,2,1,0:T(8,128)}), f32[128,2,24,8,128]{4,3,2,1,0:T(8,128)}, u32[]{:S(2)}, u32[]{:S(2)}) async-start(f32[128,2,24,8,128]{4,3,2,1,0:T(8,128)} %stack.2), calls=%async_computation | async-start | bytes 50331648 | tf_op jit(solution)/shard_map/all_to_all | solution.py:136
  238.8 4.3 collective-permute-start
  240.1 3.9 collective-permute-start.1
  246.8 147.0 %collective-permute-start.2 = (f32[24,66,1]{1,0,2:T(8,128)S(1)}, f32[24,66,1]{1,0,2:T(8,128)S(1)}, u32[]{:S(2)}, u32[]{:S(2)}) collective-permute-start(f32[24,66,1]{1,0,2:T(8,128)S(1)} %copy.133), channel_id=1, source_target_pairs={{1,0},{2,1},{3,2},{4,3},{5,4},{6,5},{7,6},{8,7},{9,8},{10,9},{11,1... | collective-permute-start | bytes 19016 | tf_op jit(solution)/shard_map/ppermute | solution.py:15
  249.3 144.8 %collective-permute-start.3 = (f32[24,66,1]{1,0,2:T(8,128)S(1)}, f32[24,66,1]{1,0,2:T(8,128)S(1)}, u32[]{:S(2)}, u32[]{:S(2)}) collective-permute-start(f32[24,66,1]{1,0,2:T(8,128)S(1)} %copy.135), channel_id=1, source_target_pairs={{0,1},{1,2},{2,3},{3,4},{4,5},{5,6},{6,7},{7,8},{8,9},{9,10},{10,1... | collective-permute-start | bytes 19016 | tf_op jit(solution)/shard_map/ppermute | solution.py:14
  399.6 210.1 %copy-start.5 = (s32[16,2]{0,1:T(2,128)S(1)}, s32[16,2]{0,1:T(2,128)}, u32[]{:S(2)}) copy-start(s32[16,2]{0,1:T(2,128)} %param.9) | copy-start | bytes 388
Sparse Core Ops, SparseCore 0:
  15.0 144.6 all-reduce.2
